TPU v7x, 256 devices: a whole 4x4x8 slice. The times are simulated.
256 devices in a mesh: grp: 16 (over y, x), tp: 16 (over z, core).
Axes of the slice: x: 4, y: 4, z: 8, core: 2. Of those that a mesh axis runs over, the one named last changes fastest.
Arguments:
- hidden: bfloat16 [294912, 5120], P(('grp', 'tp')), may hold values from -6 to 6
- lengths: int32 [16, 16], P('grp'), may hold values from 1 to 1152, 7372 in all within a row
- kv_weight: bfloat16 [5120, 1024], P('grp', 'tp'), may hold values from -0.078125 to 0.078125
- input_gain: float32 [5120], replicated, may hold values from 0.1 to 1.9
- key_gain: float32 [128], replicated, may hold values from 0.1 to 1.9
Outputs:
- cache_pages: bfloat16 [1280, 128, 1024], P(('grp', 'tp'))
Inputs may be any that keep to these rules, and one draw needn't show every extreme that they name: In each group's row the 16 lengths sum to 7372 and the largest equals 1152.
All inputs are finite; a program needn't handle non-finite values.
Results may differ from a plain program's by a relative error of at most 0.0049.
Values may be sent and summed in bfloat16 or wider, within the bound.
A program may use at most 64 MiB of HBM per device.

v0:
```python
import math
import jax
import jax.numpy as jnp
from jax import lax
from jax.sharding import PartitionSpec as P

HD = 128
KVH = 4
BLK = 128
rope_base = 1000000.0
norm_eps = 1e-06


def normalize(token_rows, input_gain):
    values = token_rows.astype(jnp.float32)
    row_scale = lax.rsqrt(jnp.mean(values * values, axis=-1, keepdims=True) + norm_eps)
    return (values * row_scale * input_gain).astype(jnp.bfloat16)


def finish(projected, positions, valid, key_gain):
    key_width = KVH * HD
    half_dim = HD // 2
    row_count = projected.shape[0]
    key_part = projected[:, :key_width].reshape(row_count, KVH, HD)
    key_scale = lax.rsqrt(jnp.mean(key_part * key_part, axis=-1, keepdims=True) + norm_eps)
    key_part = key_part * key_scale * key_gain
    exponent = jnp.arange(half_dim, dtype=jnp.float32) * (2.0 / HD)
    inverse = jnp.exp(exponent * -math.log(rope_base))
    angles = positions.astype(jnp.float32)[:, None] * inverse[None, :]
    cosine = jnp.cos(angles)[:, None, :]
    sine_part = jnp.sin(angles)[:, None, :]
    lower_half = key_part[..., :half_dim]
    upper_half = key_part[..., half_dim:]
    turned = jnp.concatenate(
        [
            lower_half * cosine - upper_half * sine_part,
            upper_half * cosine + lower_half * sine_part,
        ],
        axis=-1,
    )
    merged = jnp.concatenate(
        [turned.reshape(row_count, key_width), projected[:, key_width:]], axis=-1
    )
    return jnp.where(valid[:, None], merged, 0.0).astype(jnp.bfloat16)


def project(normed, kv_weight):
    all_rows = lax.all_gather(kv_weight, "grp", axis=0, tiled=True)
    return jnp.dot(
        normed,
        lax.all_gather(all_rows, "tp", axis=1, tiled=True),
        preferred_element_type=jnp.float32,
    )


def local(hidden, lengths, kv_weight, input_gain, key_gain):
    tp_count = lax.axis_size("tp")
    my_index = lax.axis_index("tp")
    own_blocks = hidden.shape[0] // BLK
    live_tokens = 2 * tp_count * own_blocks * BLK // 5
    page_count = ((live_tokens + BLK - 1) // BLK + 2 * tp_count - 2) // tp_count
    per_peer = (own_blocks + tp_count - 1) // tp_count
    cache_width = 2 * KVH * HD
    group_len = lengths[0]
    block_counts = (group_len + (BLK - 1)) // BLK
    block_ends = jnp.cumsum(block_counts)
    block_starts = block_ends - block_counts
    offsets = jnp.arange(BLK, dtype=jnp.int32)
    my_start = block_starts[my_index]
    my_count = block_counts[my_index]
    my_length = group_len[my_index]
    outbound = (
        jnp.arange(tp_count, dtype=jnp.int32)[:, None] - my_start
    ) % tp_count + tp_count * jnp.arange(per_peer, dtype=jnp.int32)[None, :]
    outbound = outbound.reshape(-1)
    sending = outbound < my_count
    picked_local = jnp.minimum(outbound, own_blocks - 1)
    page_ranks = tp_count * jnp.arange(page_count, dtype=jnp.int32) + my_index
    anchor = jnp.minimum(
        jnp.sum((block_ends[None, :] <= page_ranks[:, None]).astype(jnp.int32), axis=1),
        tp_count - 1,
    )
    block_index = page_ranks - block_starts[anchor]
    page_live = page_ranks < block_ends[-1]
    chosen = anchor * per_peer + jnp.clip(block_index // tp_count, 0, per_peer - 1)
    projected = project(normalize(hidden, input_gain), kv_weight)
    own_pos = (jnp.arange(own_blocks, dtype=jnp.int32)[:, None] * BLK + offsets[None, :]).reshape(
        -1
    )
    own_cache = finish(projected, own_pos, own_pos < my_length, key_gain).reshape(
        own_blocks, BLK, cache_width
    )
    outgoing = jnp.where(
        sending[:, None, None],
        jnp.take(own_cache, picked_local, axis=0),
        jnp.zeros((), jnp.bfloat16),
    )
    arrived = lax.all_to_all(outgoing, "tp", split_axis=0, concat_axis=0, tiled=True)
    cache_pages = jnp.take(arrived, chosen, axis=0)
    return jnp.where(page_live[:, None, None], cache_pages, jnp.zeros((), jnp.bfloat16))


def solution(mesh):
    placed = (P(("grp", "tp"), None), P("grp", None), P("grp", "tp"), P(), P())
    return jax.shard_map(
        local, mesh=mesh, in_specs=placed, out_specs=P(("grp", "tp"), None, None), check_vma=False
    )
```

profile of v0, /device:TPU:1, one launch (start us, length us, event | category | flops | bytes accessed | tf_op | source)
XLA Modules:
  0.0 249.6 jit_solution(15077039572765754980)
XLA Ops:
  6.5 20.4 %all-gather = bf16[16,320,64]{1,2,0:T(8,128)(2,1)S(1)} all-gather(bf16[1,320,64]{1,2,0:T(8,128)(2,1)} %bitcast.44), channel_id=1, replica_groups=mesh['grp'=16,'tp'=16] {'grp'}, dimensions={0}, use_global_device_ids=true | all-gather | bytes 696320 | tf_op jit(solution)/shard_map/all_gather | solution.py:48
  27.4 1.5 reshape.400
  31.6 1.8 compare_and_fusion
  34.0 0.6 fusion.8
  34.7 6.7 %fusion = f32[1152]{0:T(1024)S(1)} fusion(bf16[1152,5120]{1,0:T(8,128)(2,1)} %param.5), kind=kLoop, calls=%fused_computation.5 | loop fusion | flops 17693568 | bytes 11801088 | tf_op jit(solution)/shard_map/reduce_sum | solution.py:16
  41.4 3.5 %multiply_cosine_fusion = (f32[1152,64]{1,0:T(8,128)}, f32[1152,64]{1,0:T(8,128)}) fusion(f32[64]{0:T(128)S(1)} %multiply_exponential_fusion, f32[1152]{0:T(1024)S(1)} %convert_bitcast_fusion), kind=kLoop, calls=%fused_computation.21 | loop fusion | flops 73728 | bytes 594688 | tf_op jit(solution)/shard_map/cos | solution.py:30
  44.9 56.4 %all-gather.3.cloned.1.call-done = bf16[5120,1024]{0,1:T(8,128)(2,1)} async-done(((bf16[5120,64]{0,1:T(8,128)(2,1)}), bf16[5120,1024]{0,1:T(8,128)(2,1)}) %all-gather.3.cloned.1.call-update) | async-done | bytes 10485776 | tf_op jit(solution)/shard_map/all_gather | solution.py:51
  101.3 16.9 %fusion.3 = f32[1152,1024]{1,0:T(8,128)S(1)} fusion(bf16[5120,1024]{0,1:T(8,128)(2,1)} %all-gather.3.cloned.1.call-done, bf16[1152,5120]{1,0:T(8,128)(2,1)} %param.5, f32[5120]{0:T(1024)S(1)} %copy-done.8, f32[1152]{0:T(1024)S(1)} %add_rsqrt_fusion.1), kind=kOutput, calls=%fused_computation.8 | convolution fusion | flops 12103188480 | bytes 27025920 | tf_op jit(solution)/shard_map/dot_general | solution.py:49
  118.2 1.7 slice.28
  120.1 2.6 %reshape.374 = f32[1152,4,128]{2,1,0:T(4,128)S(1)} reshape(f32[1152,512]{1,0:T(8,128)} %slice.28) | data formatting | bytes 4718592 | tf_op jit(solution)/shard_map/reshape | solution.py:24
  122.7 2.0 multiply_reduce_fusion
  124.9 1.5 multiply_multiply_fusion
  126.4 1.8 multiply_subtract_fusion
  128.3 1.7 pad_maximum_fusion
  129.9 1.3 concatenate.12
  131.2 1.7 fusion.7
  132.9 2.9 %gather_fusion.1 = bf16[16,128,1024]{2,1,0:T(8,128)(2,1)} fusion(bf16[9,128,1024]{2,1,0:T(8,128)(2,1)S(1)} %fusion.7, s32[1024]{0:T(1024)} %pad_clamp_fusion.1), kind=kCustom, calls=%fused_computation.1 | custom fusion | bytes 8388672 | tf_op jit(solution)/shard_map/jit(_take)/gather | solution.py:95
  135.8 4.7 %select_select_fusion = bf16[16,128,1024]{2,1,0:T(8,128)(2,1)} fusion(bf16[16,128,1024]{2,1,0:T(8,128)(2,1)} %gather_fusion.1, pred[16]{0:T(512)(128)(4,1)S(1)} %copy-done.2, pred[16]{0:T(512)(128)(4,1)S(1)} %copy-done.3), kind=kLoop, calls=%fused_computation.13 | loop fusion | flops 4194304 | bytes 8388640 | tf_op jit(solution)/shard_map/jit(_where)/select_n | solution.py:93
  140.5 4.7 %all-to-all-start = ((bf16[16,128,1024]{2,1,0:T(8,128)(2,1)}), bf16[16,128,1024]{2,1,0:T(8,128)(2,1)}, u32[]{:S(2)}, u32[]{:S(2)}) async-start(bf16[16,128,1024]{2,1,0:T(8,128)(2,1)} %select_select_fusion), calls=%async_computation | async-start | bytes 8388608 | tf_op jit(solution)/shard_map/all_to_all | solution.py:98
  145.9 0.6 gather_fusion
  146.5 0.7 compare_and_fusion.1
  147.2 91.5 %all-to-all-done = bf16[16,128,1024]{2,1,0:T(8,128)(2,1)} async-done(((bf16[16,128,1024]{2,1,0:T(8,128)(2,1)}), bf16[16,128,1024]{2,1,0:T(8,128)(2,1)}, u32[]{:S(2)}, u32[]{:S(2)}) %all-to-all-start) | async-done | bytes 4194336 | tf_op jit(solution)/shard_map/all_to_all | solution.py:98
  238.7 2.8 %gather_fusion.2 = bf16[5,128,1024]{2,1,0:T(8,128)(2,1)S(1)} fusion(bf16[16,128,1024]{2,1,0:T(8,128)(2,1)} %all-to-all-done, s32[1024]{0:T(1024)S(1)} %pad_clamp_fusion), kind=kCustom, calls=%fused_computation.2 | custom fusion | bytes 2621460 | tf_op jit(solution)/shard_map/jit(_take)/gather | solution.py:99
  241.5 1.3 select_select_fusion.1
  (44 shorter events, 4.8 us)
Async XLA Ops:
  6.5 22.4 %copy-start.7 = (s32[1,16]{1,0:T(1,128)S(1)}, s32[1,16]{1,0:T(1,128)}, u32[]{:S(2)}) copy-start(s32[1,16]{1,0:T(1,128)} %param.6) | copy-start | bytes 196
  6.5 94.7 %all-gather.3.cloned.1.call-start = ((), (), s32[]{:S(2)}) async-start(), calls=%async_computation.1 | async-start | bytes 11141120 | tf_op jit(solution)/shard_map/all_gather | solution.py:51
  29.8 4.9 %copy-start.4 = (s32[16]{0:T(128)}, s32[16]{0:T(128)S(1)}, u32[]{:S(2)}) copy-start(s32[16]{0:T(128)S(1)} %reduce) | copy-start | bytes 196
  34.7 66.6 %copy-start.8 = (f32[5120]{0:T(1024)S(1)}, f32[5120]{0:T(1024)}, u32[]{:S(2)}) copy-start(f32[5120]{0:T(1024)} %param.8) | copy-start | bytes 61444
  122.7 2.1 copy-start.6
  124.9 1.5 copy-start
  124.9 1.5 copy-start.1
  132.9 2.9 %copy-start.2 = (pred[16]{0:T(512)(128)(4,1)S(1)}, pred[16]{0:T(512)(128)(4,1)}, u32[]{:S(2)}) copy-start(pred[16]{0:T(512)(128)(4,1)} %get-tuple-element.13) | copy-start | bytes 52
  132.9 2.9 %copy-start.3 = (pred[16]{0:T(512)(128)(4,1)S(1)}, pred[16]{0:T(512)(128)(4,1)}, u32[]{:S(2)}) copy-start(pred[16]{0:T(512)(128)(4,1)} %get-tuple-element.14) | copy-start | bytes 52
  140.5 5.2 %copy-start.5 = (s32[16]{0:T(128)S(1)}, s32[16]{0:T(128)}, u32[]{:S(2)}) copy-start(s32[16]{0:T(128)} %copy-done.4) | copy-start | bytes 196
  140.5 98.2 %all-to-all-start = ((bf16[16,128,1024]{2,1,0:T(8,128)(2,1)}), bf16[16,128,1024]{2,1,0:T(8,128)(2,1)}, u32[]{:S(2)}, u32[]{:S(2)}) async-start(bf16[16,128,1024]{2,1,0:T(8,128)(2,1)} %select_select_fusion), calls=%async_computation | async-start | bytes 8388608 | tf_op jit(solution)/shard_map/all_to_all | solution.py:98
Sparse Core Ops, SparseCore 0:
  29.1 72.1 all-gather.2
where the time goes:
time: 250 us
  waiting for transfers between devices  148 us (59%)
  other arithmetic  29.7 us (12%)
  blocking collectives  20.4 us (8%)
  matrix products  16.9 us (7%)
  local copies, waits for them, and re-layouts  16.5 us (7%)
  between operations  13.6 us (5%)
  starting transfers between devices  4.66 us (2%)
    all_to_all x1, waiting for transfers between devices, local(): lax.all_to_all(outgoing, 'tp', split_axis=0, concat_axis=0, tiled=True)  91.5 us
    all_gather x1, waiting for transfers between devices, project(): lax.all_gather(all_rows, 'tp', axis=1, tiled=True)  56.4 us
    all_gather x1, blocking collectives, project(): all_rows = lax.all_gather(kv_weight, 'grp', axis=0, tiled=True)  20.4 us
    dot_general x1, matrix products, project(): jnp.dot(normed, lax.all_gather(all_rows, 'tp', axis=1, tiled=True), prefe...  16.9 us
    reduce_sum x1, other arithmetic, normalize(): jnp.mean(values * values, axis=-1, keepdims=True) + norm_eps  6.71 us
  transfers between devices with their start and end apart: 2, of which 2 were waited for; matrix products, arithmetic and copies ran while one was open for 7% of the time, Pallas kernels for 0%

commit v1 on v0

--- a/solution.py
+++ b/solution.py
@@ -9,6 +9,18 @@
 BLK = 128
 rope_base = 1000000.0
 norm_eps = 1e-06
+
+
+def deliver_groups_up(array_dim, s0, which_axis):
+    return jnp.concatenate(
+        lax.all_to_all(
+            jnp.stack([s0] * lax.axis_size(which_axis)),
+            axis_name=which_axis,
+            split_axis=0,
+            concat_axis=0,
+        ),
+        axis=array_dim,
+    )
 
 
 def normalize(token_rows, input_gain):
@@ -46,11 +58,7 @@
 
 def project(normed, kv_weight):
     all_rows = lax.all_gather(kv_weight, "grp", axis=0, tiled=True)
-    return jnp.dot(
-        normed,
-        lax.all_gather(all_rows, "tp", axis=1, tiled=True),
-        preferred_element_type=jnp.float32,
-    )
+    return jnp.dot(normed, deliver_groups_up(1, all_rows, "tp"), preferred_element_type=jnp.float32)
 
 
 def local(hidden, lengths, kv_weight, input_gain, key_gain):

time: 250 us -> 413 us (1.65)
  waiting for transfers between devices: 148 us -> 304 us
  starting transfers between devices: 4.66 us -> 20.2 us
  between operations: 13.6 us -> 0.21 us
  local copies, waits for them, and re-layouts: 16.5 us -> 20.8 us
    all_to_all x0 -> x1, waiting for transfers between devices: none -> 212 us  [deliver_groups_up(): lax.all_to_all(jnp.stack([s0] * lax.axis_size(which_axis)), axis_name=whi...]
    all_gather x1 -> x0, waiting for transfers between devices: 56.4 us -> none  [project(): lax.all_gather(all_rows, 'tp', axis=1, tiled=True)]
    all_to_all x0 -> x1, starting transfers between devices: none -> 14.5 us  [deliver_groups_up(): lax.all_to_all(jnp.stack([s0] * lax.axis_size(which_axis)), axis_name=whi...]
    another operation x0 -> x1, local copies, waits for them, and re-layouts: none -> 5.14 us  [deliver_groups_up(): jnp.stack([s0] * lax.axis_size(which_axis))]
  transfers between devices with their start and end apart: 2 -> 2, of which waited for: 2 -> 2; matrix products, arithmetic and copies ran while one was open for 7% -> 4% of each run, Pallas kernels for 0% -> 0%
where the time goes in v1:
time: 413 us; the launch traced here: 412 us
  waiting for transfers between devices  304 us (74%)
  other arithmetic  29.9 us (7%)
  local copies, waits for them, and re-layouts  20.8 us (5%)
  blocking collectives  20.3 us (5%)
  starting transfers between devices  20.2 us (5%)
  matrix products  16.9 us (4%)
    all_to_all x1, waiting for transfers between devices, deliver_groups_up(): lax.all_to_all(jnp.stack([s0] * lax.axis_size(which_axis)), axis_name=whi...  212 us
    all_to_all x1, waiting for transfers between devices, local(): lax.all_to_all(outgoing, 'tp', split_axis=0, concat_axis=0, tiled=True)  91.4 us
    all_gather x1, blocking collectives, project(): all_rows = lax.all_gather(kv_weight, 'grp', axis=0, tiled=True)  20.3 us
    dot_general x1, matrix products, project(): jnp.dot(normed, deliver_groups_up(1, all_rows, 'tp'), preferred_element_t...  16.9 us
    all_to_all x1, starting transfers between devices, deliver_groups_up(): lax.all_to_all(jnp.stack([s0] * lax.axis_size(which_axis)), axis_name=whi...  14.5 us
  transfers between devices with their start and end apart: 2, of which 2 were waited for; matrix products, arithmetic and copies ran while one was open for 4% of the time, Pallas kernels for 0%

profile of v1, /device:TPU:1, one launch (start us, length us, event | category | flops | bytes accessed | tf_op | source)
XLA Modules:
  0.0 412.1 jit_solution(11193927119710140460)
XLA Ops:
  0.0 20.3 %all-gather = bf16[16,320,64]{1,2,0:T(8,128)(2,1)S(1)} all-gather(bf16[1,320,64]{1,2,0:T(8,128)(2,1)} %bitcast.47), channel_id=1, replica_groups=mesh['grp'=16,'tp'=16] {'grp'}, dimensions={0}, use_global_device_ids=true | all-gather | bytes 696320 | tf_op jit(solution)/shard_map/all_gather | solution.py:60
  21.4 5.1 %stack.2 = bf16[16,5120,64]{1,2,0:T(8,128)(2,1)} broadcast(bf16[5120,64]{0,1:T(8,128)(2,1)S(1)} %reshape.410), dimensions={1,2} | broadcast | bytes 11141120 | tf_op jit(solution)/shard_map/stack | solution.py:17
  26.5 14.5 %all-to-all-start = ((bf16[16,5120,64]{1,2,0:T(8,128)(2,1)}), bf16[16,5120,64]{1,2,0:T(8,128)(2,1)}, u32[]{:S(2)}, u32[]{:S(2)}) async-start(bf16[16,5120,64]{1,2,0:T(8,128)(2,1)} %stack.2), calls=%async_computation | async-start | bytes 20971520 | tf_op jit(solution)/shard_map/all_to_all | solution.py:16
  43.1 0.7 fusion.13
  43.8 1.8 compare_and_fusion
  46.2 0.7 fusion.8
  47.0 6.7 %fusion = f32[1152]{0:T(1024)S(1)} fusion(bf16[1152,5120]{1,0:T(8,128)(2,1)} %param.5), kind=kLoop, calls=%fused_computation.5 | loop fusion | flops 17693568 | bytes 11801088 | tf_op jit(solution)/shard_map/reduce_sum | solution.py:28
  53.7 3.2 multiply_cosine_fusion
  57.0 212.4 %all-to-all-done = bf16[16,5120,64]{1,2,0:T(8,128)(2,1)} async-done(((bf16[16,5120,64]{1,2,0:T(8,128)(2,1)}), bf16[16,5120,64]{1,2,0:T(8,128)(2,1)}, u32[]{:S(2)}, u32[]{:S(2)}) %all-to-all-start) | async-done | bytes 10485792 | tf_op jit(solution)/shard_map/all_to_all | solution.py:16
  269.3 16.9 %fusion.3 = f32[1152,1024]{1,0:T(8,128)S(1)} fusion(bf16[5120,1024]{0,1:T(8,128)(2,1)} %bitcast.10, bf16[1152,5120]{1,0:T(8,128)(2,1)} %param.5, f32[5120]{0:T(1024)S(1)} %copy-done.8, f32[1152]{0:T(1024)S(1)} %add_rsqrt_fusion.1), kind=kOutput, calls=%fused_computation.8 | convolution fusion | flops 12103188480 | bytes 27025920 | tf_op jit(solution)/shard_map/dot_general | solution.py:61
  286.3 1.7 slice.28
  288.1 2.6 reshape.384
  290.8 2.0 multiply_reduce_fusion
  292.9 1.5 multiply_multiply_fusion
  294.5 1.8 multiply_subtract_fusion
  296.3 1.9 pad_maximum_fusion
  298.2 1.3 concatenate.12
  299.5 1.7 fusion.7
  301.2 2.9 gather_fusion.1
  304.1 4.7 %select_select_fusion = bf16[16,128,1024]{2,1,0:T(8,128)(2,1)} fusion(bf16[16,128,1024]{2,1,0:T(8,128)(2,1)} %gather_fusion.1, pred[16]{0:T(512)(128)(4,1)S(1)} %copy-done.2, pred[16]{0:T(512)(128)(4,1)S(1)} %copy-done.3), kind=kLoop, calls=%fused_computation.13 | loop fusion | flops 4194304 | bytes 8388640 | tf_op jit(solution)/shard_map/jit(_where)/select_n | solution.py:101
  308.8 5.8 %all-to-all-start.1 = ((bf16[16,128,1024]{2,1,0:T(8,128)(2,1)}), bf16[16,128,1024]{2,1,0:T(8,128)(2,1)}, u32[]{:S(2)}, u32[]{:S(2)}) async-start(bf16[16,128,1024]{2,1,0:T(8,128)(2,1)} %select_select_fusion), calls=%async_computation.1 | async-start | bytes 8388608 | tf_op jit(solution)/shard_map/all_to_all | solution.py:106
  316.6 91.4 %all-to-all-done.1 = bf16[16,128,1024]{2,1,0:T(8,128)(2,1)} async-done(((bf16[16,128,1024]{2,1,0:T(8,128)(2,1)}), bf16[16,128,1024]{2,1,0:T(8,128)(2,1)}, u32[]{:S(2)}, u32[]{:S(2)}) %all-to-all-start.1) | async-done | bytes 4194336 | tf_op jit(solution)/shard_map/all_to_all | solution.py:106
  408.0 2.8 gather_fusion.2
  410.9 1.3 select_select_fusion.1
  (44 shorter events, 6.2 us)
Async XLA Ops:
  26.5 14.5 %copy-start.7 = (s32[1,16]{1,0:T(1,128)S(1)}, s32[1,16]{1,0:T(1,128)}, u32[]{:S(2)}) copy-start(s32[1,16]{1,0:T(1,128)} %param.6) | copy-start | bytes 196
  26.5 242.8 %all-to-all-start = ((bf16[16,5120,64]{1,2,0:T(8,128)(2,1)}), bf16[16,5120,64]{1,2,0:T(8,128)(2,1)}, u32[]{:S(2)}, u32[]{:S(2)}) async-start(bf16[16,5120,64]{1,2,0:T(8,128)(2,1)} %stack.2), calls=%async_computation | async-start | bytes 20971520 | tf_op jit(solution)/shard_map/all_to_all | solution.py:16
  41.8 5.2 %copy-start.4 = (s32[16]{0:T(128)}, s32[16]{0:T(128)S(1)}, u32[]{:S(2)}) copy-start(s32[16]{0:T(128)S(1)} %reduce) | copy-start | bytes 196
  47.0 222.3 %copy-start.8 = (f32[5120]{0:T(1024)S(1)}, f32[5120]{0:T(1024)}, u32[]{:S(2)}) copy-start(f32[5120]{0:T(1024)} %param.8) | copy-start | bytes 61444
  290.8 2.1 copy-start.6
  292.9 1.5 copy-start
  292.9 1.5 copy-start.1
  301.2 2.9 copy-start.2
  301.2 2.9 copy-start.3
  308.8 6.3 %copy-start.5 = (s32[16]{0:T(128)S(1)}, s32[16]{0:T(128)}, u32[]{:S(2)}) copy-start(s32[16]{0:T(128)} %copy-done.4) | copy-start | bytes 196
  308.8 99.3 %all-to-all-start.1 = ((bf16[16,128,1024]{2,1,0:T(8,128)(2,1)}), bf16[16,128,1024]{2,1,0:T(8,128)(2,1)}, u32[]{:S(2)}, u32[]{:S(2)}) async-start(bf16[16,128,1024]{2,1,0:T(8,128)(2,1)} %select_select_fusion), calls=%async_computation.1 | async-start | bytes 8388608 | tf_op jit(solution)/shard_map/all_to_all | solution.py:106
